TPU v7x, 512 devices: a whole 4x4x16 slice. The times are simulated.
512 devices in a mesh: row: 16 (over x_hi, y, core), col: 32 (over z, x_lo).
Axes of the slice: x: 4 (x_hi: 2, x_lo: 2; x = x_hi * 2 + x_lo), y: 4, z: 16, core: 2. Of those that a mesh axis runs over, the one named last changes fastest.
Arguments:
- orbitals: bfloat16 [16384, 2048], P(('row', 'col')), may hold values from -0.125 to 0.125
- coulomb: bfloat16 [16384, 16384], P('row', 'col'), may hold values from -6 to 6
- applied: bfloat16 [16384, 256], P(('row', 'col')), may hold values from -6 to 6
Outputs:
- projectors: float32 [16384, 256], P(('row', 'col'))
All inputs are finite; a program needn't handle non-finite values.
Results may differ from a plain program's by a relative error of at most 0.0029.
Values may be sent and summed in bfloat16 or wider, within the bound.
No kernel may reach another device: no remote copies, remote signals or barrier semaphores. Data moves between devices by JAX's collectives and lax.ppermute only.
A program may use at most 64 MiB of HBM per device.

v0:
```python
import jax
import jax.numpy as jnp
from jax import lax
from jax.sharding import PartitionSpec as P

NMU = 16384


def per_device(orbitals, coulomb, applied):
    point_block = lax.all_gather(orbitals, "col", axis=0, tiled=True)
    paired_orbitals, paired_applied = (
        lax.all_gather(orbitals, "row", axis=0, tiled=True),
        lax.all_gather(applied, "row", axis=0, tiled=True),
    )
    density = jnp.einsum(
        "ik,jk->ij", point_block, paired_orbitals, preferred_element_type=jnp.float32
    )
    kernel = (coulomb.astype(jnp.float32) * density).astype(jnp.bfloat16)
    images = lax.psum_scatter(
        jnp.dot(kernel, paired_applied, preferred_element_type=jnp.float32),
        "col",
        scatter_dimension=0,
        tiled=True,
    )
    local_gram = jnp.einsum("ia,ib->ab", images, images, precision=lax.Precision.HIGHEST)
    gram_sum = lax.psum(local_gram, ("row", "col"))
    gram_matrix = jnp.eye(gram_sum.shape[0], dtype=jnp.float32) + gram_sum / NMU
    factor = jnp.linalg.cholesky(gram_matrix)
    projectors = lax.linalg.triangular_solve(
        factor, images, left_side=False, lower=True, transpose_a=True
    )
    return projectors


def solution(mesh):
    return jax.shard_map(
        per_device,
        mesh=mesh,
        in_specs=(P(("row", "col"), None), P("row", "col"), P(("row", "col"), None)),
        out_specs=P(("row", "col"), None),
        check_vma=False,
    )
```

profile of v0, /device:TPU:4, one launch (start us, length us, event | category | flops | bytes accessed | tf_op | source)
XLA Modules:
  0.0 898.7 jit_solution(3592845915459076260)
XLA Ops:
  6.5 0.7 all-gather.5.cloned.1.call-update
  7.3 0.7 all-gather.3.cloned.1.call-update
  8.1 22.8 %all_gather.11 = bf16[512,256]{1,0:T(8,128)(2,1)S(1)} all-gather(bf16[32,256]{1,0:T(8,128)(2,1)} %param.5), channel_id=1, replica_groups=mesh['row'=16,'col'=32] {'row'}, dimensions={0}, use_global_device_ids=true | all-gather | bytes 278528 | tf_op jit(solution)/shard_map/all_gather | solution.py:13
  30.9 44.7 %all-gather.5.cloned.1.call-done = bf16[512,2048]{1,0:T(8,128)(2,1)} async-done(((bf16[32,2048]{1,0:T(8,128)(2,1)}), bf16[512,2048]{1,0:T(8,128)(2,1)}) %all-gather.5.cloned.1.call-update) | async-done | bytes 2097168 | tf_op jit(solution)/shard_map/all_gather | solution.py:12
  75.6 143.3 %all-gather.3.cloned.1.call-done = bf16[1024,2048]{1,0:T(8,128)(2,1)} async-done(((bf16[32,2048]{1,0:T(8,128)(2,1)}), bf16[1024,2048]{1,0:T(8,128)(2,1)}) %all-gather.3.cloned.1.call-update) | async-done | bytes 4194320 | tf_op jit(solution)/shard_map/all_gather | solution.py:10
  218.8 6.8 fusion
  225.7 0.2 all-reduce.3.cloned.1.call-start
  225.9 134.5 %reduce-scatter.2.cloned.1.call-done = f32[32,256]{1,0:T(8,128)} async-done(((f32[1024,256]{1,0:T(8,128)}), f32[32,256]{1,0:T(8,128)}) %reduce-scatter.2.cloned.1.call-update) | async-done | bytes 32784 | tf_op jit(solution)/shard_map/reduce_scatter | solution.py:19
  360.4 1.9 fusion.10
  362.4 466.6 %all-reduce.3.cloned.1.call-done = f32[256,256]{0,1:T(8,128)} async-done(((f32[256,256]{0,1:T(8,128)}), f32[256,256]{0,1:T(8,128)}) %all-reduce.3.cloned.1.call-update) | async-done | bytes 262160 | tf_op jit(solution)/shard_map/psum | solution.py:26
  829.0 1.0 multiply_add_fusion
  830.2 1.0 fusion.1
  831.2 11.7 %cholesky.50 = f32[128,128]{1,0:T(8,128)S(1)} custom-call(f32[128,128]{1,0:T(8,128)S(1)} %cholesky.118), custom_call_target="Cholesky" | custom-call | tf_op jit(solution)/shard_map/jit(cholesky)/cholesky | solution.py:28
  842.9 9.8 %custom-call.14 = f32[1,128,128]{1,2,0:T(8,128)S(1)} custom-call(f32[1,128,128]{2,1,0:T(8,128)S(1)} %get-tuple-element.26), custom_call_target="InvertDiagBlocksLowerTriangular" | custom-call | tf_op jit(solution)/shard_map/jit(cholesky)/cholesky | solution.py:28
  853.0 0.3 convolution_subtract_fusion
  853.3 11.7 %cholesky.105 = f32[128,128]{1,0:T(8,128)S(1)} custom-call(f32[128,128]{1,0:T(8,128)S(1)} %convolution_subtract_fusion), custom_call_target="Cholesky" | custom-call | tf_op jit(solution)/shard_map/jit(cholesky)/cholesky | solution.py:28
  865.0 0.7 compare_reduce_fusion
  867.1 4.2 while.1
  867.3 0.6 fusion.21
  867.9 1.4 bitcast_dynamic-update-slice_fusion.2
  869.3 0.6 fusion.21
  869.9 1.4 bitcast_dynamic-update-slice_fusion.2
  871.3 19.7 %custom-call.15 = f32[2,128,128]{1,2,0:T(8,128)S(1)} custom-call(f32[2,128,128]{2,1,0:T(8,128)S(1)} %get-tuple-element.12), custom_call_target="InvertDiagBlocksLowerTriangular" | custom-call | tf_op jit(solution)/shard_map/triangular_solve | solution.py:29
  891.5 0.6 pad_maximum_fusion
  (22 shorter events, 1.2 us)
Async XLA Ops:
  6.5 69.0 %all-gather.5.cloned.1.call-start = ((), (), s32[]{:S(2)}) async-start(), calls=%async_computation.2 | async-start | bytes 2228224 | tf_op jit(solution)/shard_map/all_gather | solution.py:12
  7.3 211.6 %all-gather.3.cloned.1.call-start = ((), (), s32[]{:S(2)}) async-start(), calls=%async_computation.1 | async-start | bytes 4325376 | tf_op jit(solution)/shard_map/all_gather | solution.py:10
  8.0 352.4 %reduce-scatter.2.cloned.1.call-start = ((), (), s32[]{:S(2)}) async-start(), calls=%async_computation.3 | async-start | bytes 1081344 | tf_op jit(solution)/shard_map/reduce_scatter | solution.py:19
  225.7 603.4 %all-reduce.3.cloned.1.call-start = ((), (), s32[]{:S(2)}) async-start(), calls=%async_computation.4 | async-start | bytes 524288 | tf_op jit(solution)/shard_map/psum | solution.py:26
  830.0 60.9 %copy-start = (f32[32,256]{1,0:T(8,128)S(1)}, f32[32,256]{1,0:T(8,128)}, u32[]{:S(2)}) copy-start(f32[32,256]{1,0:T(8,128)} %reduce-scatter.2.cloned.1.call-done) | copy-start | bytes 98308
Sparse Core Ops, SparseCore 0:
  10.7 64.8 all-gather.4
  77.6 141.1 all-gather.2
  225.8 134.5 reduce-scatter.1
  365.7 463.2 all-reduce.2
where the time goes:
time: 899 us
  waiting for transfers between devices  791 us (88%)
  other arithmetic  56.3 us (6%)
  blocking collectives  22.8 us (3%)
  between operations  14.5 us (2%)
  matrix products  9.77 us (1%)
    psum x1, waiting for transfers between devices, per_device(): gram_sum = lax.psum(local_gram, ('row', 'col'))  467 us
    all_gather x1, waiting for transfers between devices, per_device(): point_block = lax.all_gather(orbitals, 'col', axis=0, tiled=True)  143 us
    reduce_scatter x1, waiting for transfers between devices, per_device(): lax.psum_scatter(jnp.dot(kernel, paired_applied, preferred_element_type=j...  135 us
    all_gather x1, waiting for transfers between devices, per_device(): lax.all_gather(orbitals, 'row', axis=0, tiled=True)  44.7 us
    another operation x6, other arithmetic, per_device(): factor = jnp.linalg.cholesky(gram_matrix)  34 us
    all_gather x1, blocking collectives, per_device(): lax.all_gather(applied, 'row', axis=0, tiled=True)  22.8 us
    another operation x4, other arithmetic, per_device(): lax.linalg.triangular_solve(factor, images, left_side=False, lower=True,...  20.3 us
  transfers between devices with their start and end apart: 4, of which 4 were waited for; matrix products, arithmetic and copies ran while one was open for 0% of the time, Pallas kernels for 0%

commit v1 on v0

--- a/solution.py
+++ b/solution.py
@@ -23,7 +23,7 @@
         tiled=True,
     )
     local_gram = jnp.einsum("ia,ib->ab", images, images, precision=lax.Precision.HIGHEST)
-    gram_sum = lax.psum(local_gram, ("row", "col"))
+    gram_sum = lax.psum(lax.psum(local_gram, "row"), "col")
     gram_matrix = jnp.eye(gram_sum.shape[0], dtype=jnp.float32) + gram_sum / NMU
     factor = jnp.linalg.cholesky(gram_matrix)
     projectors = lax.linalg.triangular_solve(

time: 899 us -> 854 us (0.950)
  the two profiles are of different devices: /device:TPU:4 before, /device:TPU:8 now
where the time goes in v1:
time: 854 us
  waiting for transfers between devices  743 us (87%)
  other arithmetic  56.3 us (7%)
  blocking collectives  25.6 us (3%)
  between operations  14.5 us (2%)
  matrix products  9.77 us (1%)
    psum x2, waiting for transfers between devices, per_device(): gram_sum = lax.psum(lax.psum(local_gram, 'row'), 'col')  421 us
    all_gather x1, waiting for transfers between devices, per_device(): point_block = lax.all_gather(orbitals, 'col', axis=0, tiled=True)  141 us
    reduce_scatter x1, waiting for transfers between devices, per_device(): lax.psum_scatter(jnp.dot(kernel, paired_applied, preferred_element_type=j...  135 us
    all_gather x1, waiting for transfers between devices, per_device(): lax.all_gather(orbitals, 'row', axis=0, tiled=True)  44 us
    another operation x6, other arithmetic, per_device(): factor = jnp.linalg.cholesky(gram_matrix)  34 us
    all_gather x1, blocking collectives, per_device(): lax.all_gather(applied, 'row', axis=0, tiled=True)  25.6 us
    another operation x4, other arithmetic, per_device(): lax.linalg.triangular_solve(factor, images, left_side=False, lower=True,...  20.3 us
  transfers between devices with their start and end apart: 5, of which 5 were waited for; matrix products, arithmetic and copies ran while one was open for 0% of the time, Pallas kernels for 0%

profile of v1, /device:TPU:8, one launch (start us, length us, event | category | flops | bytes accessed | tf_op | source)
XLA Modules:
  0.0 853.9 jit_solution(14866419415546281674)
XLA Ops:
  6.5 0.7 all-gather.5.cloned.1.call-update
  7.3 0.7 all-gather.3.cloned.1.call-update
  8.1 25.6 %all_gather.11 = bf16[512,256]{1,0:T(8,128)(2,1)S(1)} all-gather(bf16[32,256]{1,0:T(8,128)(2,1)} %param.5), channel_id=1, replica_groups=mesh['row'=16,'col'=32] {'row'}, dimensions={0}, use_global_device_ids=true | all-gather | bytes 278528 | tf_op jit(solution)/shard_map/all_gather | solution.py:13
  33.7 44.0 %all-gather.5.cloned.1.call-done = bf16[512,2048]{1,0:T(8,128)(2,1)} async-done(((bf16[32,2048]{1,0:T(8,128)(2,1)}), bf16[512,2048]{1,0:T(8,128)(2,1)}) %all-gather.5.cloned.1.call-update) | async-done | bytes 2097168 | tf_op jit(solution)/shard_map/all_gather | solution.py:12
  77.7 141.3 %all-gather.3.cloned.1.call-done = bf16[1024,2048]{1,0:T(8,128)(2,1)} async-done(((bf16[32,2048]{1,0:T(8,128)(2,1)}), bf16[1024,2048]{1,0:T(8,128)(2,1)}) %all-gather.3.cloned.1.call-update) | async-done | bytes 4194320 | tf_op jit(solution)/shard_map/all_gather | solution.py:10
  218.9 6.8 fusion
  225.8 135.1 %reduce-scatter.2.cloned.1.call-done = f32[32,256]{1,0:T(8,128)} async-done(((f32[1024,256]{1,0:T(8,128)}), f32[32,256]{1,0:T(8,128)}) %reduce-scatter.2.cloned.1.call-update) | async-done | bytes 32784 | tf_op jit(solution)/shard_map/reduce_scatter | solution.py:19
  360.9 1.9 fusion.10
  363.1 148.3 %all-reduce.4.cloned.1.call-done = f32[256,256]{0,1:T(8,128)} async-done(((f32[256,256]{0,1:T(8,128)}), f32[256,256]{0,1:T(8,128)}) %all-reduce.4.cloned.1.call-update) | async-done | bytes 262160 | tf_op jit(solution)/shard_map/psum | solution.py:26
  511.4 272.9 %all-reduce.6.cloned.1.call-done = f32[256,256]{0,1:T(8,128)} async-done(((f32[256,256]{0,1:T(8,128)}), f32[256,256]{0,1:T(8,128)}) %all-reduce.6.cloned.1.call-update) | async-done | bytes 262160 | tf_op jit(solution)/shard_map/psum | solution.py:26
  784.3 1.0 multiply_add_fusion
  785.4 1.0 fusion.1
  786.4 11.7 %cholesky.50 = f32[128,128]{1,0:T(8,128)S(1)} custom-call(f32[128,128]{1,0:T(8,128)S(1)} %cholesky.118), custom_call_target="Cholesky" | custom-call | tf_op jit(solution)/shard_map/jit(cholesky)/cholesky | solution.py:28
  798.2 9.8 %custom-call.14 = f32[1,128,128]{1,2,0:T(8,128)S(1)} custom-call(f32[1,128,128]{2,1,0:T(8,128)S(1)} %get-tuple-element.26), custom_call_target="InvertDiagBlocksLowerTriangular" | custom-call | tf_op jit(solution)/shard_map/jit(cholesky)/cholesky | solution.py:28
  808.2 0.3 convolution_subtract_fusion
  808.5 11.7 %cholesky.105 = f32[128,128]{1,0:T(8,128)S(1)} custom-call(f32[128,128]{1,0:T(8,128)S(1)} %convolution_subtract_fusion), custom_call_target="Cholesky" | custom-call | tf_op jit(solution)/shard_map/jit(cholesky)/cholesky | solution.py:28
  820.2 0.7 compare_reduce_fusion
  822.3 4.2 while.1
  822.5 0.6 fusion.21
  823.1 1.4 bitcast_dynamic-update-slice_fusion.2
  824.5 0.6 fusion.21
  825.1 1.4 bitcast_dynamic-update-slice_fusion.2
  826.5 19.7 %custom-call.15 = f32[2,128,128]{1,2,0:T(8,128)S(1)} custom-call(f32[2,128,128]{2,1,0:T(8,128)S(1)} %get-tuple-element.12), custom_call_target="InvertDiagBlocksLowerTriangular" | custom-call | tf_op jit(solution)/shard_map/triangular_solve | solution.py:29
  846.7 0.6 pad_maximum_fusion
  (25 shorter events, 1.5 us)
Async XLA Ops:
  6.5 71.1 %all-gather.5.cloned.1.call-start = ((), (), s32[]{:S(2)}) async-start(), calls=%async_computation.2 | async-start | bytes 2228224 | tf_op jit(solution)/shard_map/all_gather | solution.py:12
  7.3 211.7 %all-gather.3.cloned.1.call-start = ((), (), s32[]{:S(2)}) async-start(), calls=%async_computation.1 | async-start | bytes 4325376 | tf_op jit(solution)/shard_map/all_gather | solution.py:10
  8.0 352.9 %reduce-scatter.2.cloned.1.call-start = ((), (), s32[]{:S(2)}) async-start(), calls=%async_computation.3 | async-start | bytes 1081344 | tf_op jit(solution)/shard_map/reduce_scatter | solution.py:19
  225.8 285.6 %all-reduce.4.cloned.1.call-start = ((), (), s32[]{:S(2)}) async-start(), calls=%async_computation.4 | async-start | bytes 524288 | tf_op jit(solution)/shard_map/psum | solution.py:26
  362.8 421.4 %all-reduce.6.cloned.1.call-start = ((), (), s32[]{:S(2)}) async-start(), calls=%async_computation.5 | async-start | bytes 524288 | tf_op jit(solution)/shard_map/psum | solution.py:26
  785.2 60.9 %copy-start = (f32[32,256]{1,0:T(8,128)S(1)}, f32[32,256]{1,0:T(8,128)}, u32[]{:S(2)}) copy-start(f32[32,256]{1,0:T(8,128)} %reduce-scatter.2.cloned.1.call-done) | copy-start | bytes 98308
Sparse Core Ops, SparseCore 0:
  10.7 66.9 all-gather.4
  79.7 139.1 all-gather.2
  225.9 134.9 reduce-scatter.1
  363.6 147.6 all-reduce.3
  514.1 270.1 all-reduce.5
